TPU v7x, 256 devices: a whole 4x4x8 slice. The times are simulated.
256 devices in a mesh: dp: 8 (over x, z_hi), tensor: 8 (over y, core), expert: 4 (over z_lo).
Axes of the slice: x: 4, y: 4, z: 8 (z_hi: 2, z_lo: 4; z = z_hi * 4 + z_lo), core: 2. Of those that a mesh axis runs over, the one named last changes fastest.
Arguments:
- moe_input: bfloat16 [8192, 2048], P(('dp', 'tensor'), 'expert'), may hold values from -6 to 6
- grad_output: bfloat16 [8192, 2048], P(('dp', 'tensor'), 'expert'), may hold values from -6 to 6
- routes: int32 [8192, 8], P(('dp', 'tensor')), may hold values from 0 to 127, all different within a row; in each aligned block of 128 rows (0 to 127, 128 to 255, ...) at most 12 rows name the same one
- route_weight: float32 [8192, 8], P(('dp', 'tensor')), may hold values from 0.05 to 0.35
- capacity: int32 [128], replicated, may hold values from 6 to 12, as said below
- w_gate: bfloat16 [256, 384, 2048], P(('dp', 'tensor', 'expert')), may hold values from -0.125 to 0.125
- w_up: bfloat16 [256, 384, 2048], P(('dp', 'tensor', 'expert')), may hold values from -0.125 to 0.125
- w_down: bfloat16 [256, 384, 2048], P(('dp', 'tensor', 'expert')), may hold values from -0.21875 to 0.21875
Outputs:
- moe_output: bfloat16 [8192, 2048], P(('dp', 'tensor'), 'expert')
- grad_input: bfloat16 [8192, 2048], P(('dp', 'tensor'), 'expert')
- grad_gate: bfloat16 [256, 384, 2048], P(('dp', 'tensor', 'expert'))
- grad_up: bfloat16 [256, 384, 2048], P(('dp', 'tensor', 'expert'))
- grad_down: bfloat16 [256, 384, 2048], P(('dp', 'tensor', 'expert'))
Inputs may be any that keep to these rules, and one draw needn't show every extreme that they name: `routes`: each row names 8 different experts; within each aligned block of 128 rows (the rows of one device) no expert is named more than 12 times. Some expert has a capacity of exactly 12.
All inputs are finite; a program needn't handle non-finite values.
Results may differ from a plain program's by a relative error of at most 0.0071.
Values may be sent and summed in bfloat16 or wider, within the bound.
A program may use at most 128 MiB of HBM per device.

v0:
```python
import jax
import jax.numpy as jnp
from jax import lax
from jax.sharding import PartitionSpec as P


def swapped(x, axis, apart):
    return lax.ppermute(x, axis, [(i, i ^ 1 << apart) for i in range(lax.axis_size(axis))])


def expert_work(slot_rows, slot_cots, gate_w, up_w, down_w):
    gate_pre = jnp.einsum("smd,hd->smh", slot_rows, gate_w, preferred_element_type=jnp.float32)
    up_pre = jnp.einsum("smd,hd->smh", slot_rows, up_w, preferred_element_type=jnp.float32)
    sigmoid_gate = jax.nn.sigmoid(gate_pre)
    gate_act = gate_pre * sigmoid_gate
    hidden = (gate_act * up_pre).astype(jnp.bfloat16)
    out_part = jnp.einsum("smh,hd->smd", hidden, down_w, preferred_element_type=jnp.float32).astype(
        jnp.bfloat16
    )
    hidden_cot = jnp.einsum("smd,hd->smh", slot_cots, down_w, preferred_element_type=jnp.float32)
    gate_cot = (
        hidden_cot * up_pre * sigmoid_gate * (1.0 + gate_pre * (1.0 - sigmoid_gate))
    ).astype(jnp.bfloat16)
    up_cot = (hidden_cot * gate_act).astype(jnp.bfloat16)
    in_sum = jnp.einsum("smh,hd->smd", gate_cot, gate_w, preferred_element_type=jnp.float32)
    in_sum = in_sum + jnp.einsum("smh,hd->smd", up_cot, up_w, preferred_element_type=jnp.float32)
    in_part = in_sum.astype(jnp.bfloat16)
    grad_gate = jnp.einsum(
        "smh,smd->hd", gate_cot, slot_rows, preferred_element_type=jnp.float32
    ).astype(jnp.bfloat16)
    grad_up = jnp.einsum(
        "smh,smd->hd", up_cot, slot_rows, preferred_element_type=jnp.float32
    ).astype(jnp.bfloat16)
    grad_down = jnp.einsum(
        "smh,smd->hd", hidden, slot_cots, preferred_element_type=jnp.float32
    ).astype(jnp.bfloat16)
    return (out_part, in_part, grad_gate[None], grad_up[None], grad_down[None])


def fill_slots(inputs, cots, owners, weights):
    filled = owners >= 0
    source = jnp.maximum(owners, 0)
    slot_rows = jnp.where(filled[..., None], inputs[source], jnp.zeros((), inputs.dtype))
    slot_cots = jnp.where(
        filled[..., None], weights[..., None] * cots[source].astype(jnp.float32), 0.0
    )
    return (slot_rows, slot_cots.astype(jnp.bfloat16))


def shards(moe_input, grad_output, routes, route_weight, capacity, w_gate, w_up, w_down):
    groups = lax.axis_size(("dp", "tensor"))
    position = lax.axis_index("expert")
    parity = position // 2
    half_index = position % 2
    tok_rows = routes.shape[0]
    topk = routes.shape[1]
    experts = capacity.shape[0]
    slot_depth = 12 * tok_rows // experts
    slot_count = experts * slot_depth
    pair_count = tok_rows * topk
    col_quarter = moe_input.shape[1]
    full_width = col_quarter * lax.axis_size("expert")
    half_width = full_width // 2
    flat_routes = routes.reshape(pair_count)
    onehot = (flat_routes[:, None] == jnp.arange(experts, dtype=jnp.int32)[None, :]).astype(
        jnp.int32
    )
    before = jnp.cumsum(onehot, axis=0) - onehot
    pair_rank = jnp.sum(onehot * before, axis=1)
    pair_limit = jnp.sum(onehot * capacity[None, :], axis=1)
    pair_kept = pair_rank < pair_limit
    pair_place = jnp.where(pair_kept, flat_routes * slot_depth + pair_rank, slot_count)
    pair_token = jnp.arange(pair_count, dtype=jnp.int32) // topk
    flat_weight = route_weight.reshape(pair_count)
    slot_owner = jnp.full((slot_count,), -1, jnp.int32).at[pair_place].set(pair_token, mode="drop")
    slot_weight = jnp.zeros((slot_count,), jnp.float32).at[pair_place].set(flat_weight, mode="drop")
    whole_input, whole_cot = (
        lax.all_gather(moe_input, "expert", axis=1, tiled=True),
        lax.all_gather(grad_output, "expert", axis=1, tiled=True),
    )
    owners = lax.dynamic_index_in_dim(
        slot_owner.reshape(groups, 2, slot_depth), parity, 1, keepdims=False
    )
    weights = lax.dynamic_index_in_dim(
        slot_weight.reshape(groups, 2, slot_depth), parity, 1, keepdims=False
    )
    send_rows, send_cots = fill_slots(whole_input, whole_cot, owners, weights)
    got_rows, got_cots = (
        lax.all_to_all(send_rows, ("dp", "tensor"), split_axis=0, concat_axis=0, tiled=True),
        lax.all_to_all(send_cots, ("dp", "tensor"), split_axis=0, concat_axis=0, tiled=True),
    )
    out_part, in_part, grad_gate, grad_up, grad_down = expert_work(
        got_rows, got_cots, w_gate[0], w_up[0], w_down[0]
    )
    out_split = out_part.reshape(groups, slot_depth, 2, half_width)
    in_split = in_part.reshape(groups, slot_depth, 2, half_width)
    mine_out = lax.dynamic_index_in_dim(out_split, half_index, 2, keepdims=False)
    mine_in = lax.dynamic_index_in_dim(in_split, half_index, 2, keepdims=False)
    other_out = lax.dynamic_index_in_dim(out_split, 1 - half_index, 2, keepdims=False)
    other_in = lax.dynamic_index_in_dim(in_split, 1 - half_index, 2, keepdims=False)
    peer_out, peer_in = swapped((other_out, other_in), "expert", 0)
    expert_out = (mine_out.astype(jnp.float32) + peer_out.astype(jnp.float32)).astype(jnp.bfloat16)
    input_slot = (mine_in.astype(jnp.float32) + peer_in.astype(jnp.float32)).astype(jnp.bfloat16)
    back_out, back_in = (
        lax.all_to_all(expert_out, ("dp", "tensor"), split_axis=0, concat_axis=0, tiled=True),
        lax.all_to_all(input_slot, ("dp", "tensor"), split_axis=0, concat_axis=0, tiled=True),
    )
    flat_out = back_out.reshape(groups * slot_depth, half_width)
    flat_in = back_in.reshape(groups * slot_depth, half_width)
    matched = pair_kept & (flat_routes % 2 == parity)
    back_place = jnp.where(matched, flat_routes // 2 * slot_depth + pair_rank, 0)
    pair_scale = jnp.where(matched, flat_weight, 0.0)
    pair_mask = jnp.where(matched, 1.0, 0.0)
    partial_out = jnp.sum(
        (flat_out[back_place].astype(jnp.float32) * pair_scale[:, None]).reshape(
            tok_rows, topk, half_width
        ),
        axis=1,
    )
    partial_in = jnp.sum(
        (flat_in[back_place].astype(jnp.float32) * pair_mask[:, None]).reshape(
            tok_rows, topk, half_width
        ),
        axis=1,
    )
    which_half = (jnp.arange(2, dtype=jnp.int32) == half_index)[None, :, None]
    placed_out = jnp.where(which_half, partial_out[:, None, :], 0.0).reshape(tok_rows, full_width)
    placed_in = jnp.where(which_half, partial_in[:, None, :], 0.0).reshape(tok_rows, full_width)
    moe_output, grad_input = (
        lax.psum_scatter(placed_out, "expert", scatter_dimension=1, tiled=True),
        lax.psum_scatter(placed_in, "expert", scatter_dimension=1, tiled=True),
    )
    return (
        moe_output.astype(jnp.bfloat16),
        grad_input.astype(jnp.bfloat16),
        grad_gate,
        grad_up,
        grad_down,
    )


def solution(mesh):
    in_specs = (
        P(("dp", "tensor"), "expert"),
        P(("dp", "tensor"), "expert"),
        P(("dp", "tensor"), None),
        P(("dp", "tensor"), None),
        P(),
        P(("dp", "tensor", "expert"), None, None),
        P(("dp", "tensor", "expert"), None, None),
        P(("dp", "tensor", "expert"), None, None),
    )
    out_specs = (
        P(("dp", "tensor"), "expert"),
        P(("dp", "tensor"), "expert"),
        P(("dp", "tensor", "expert"), None, None),
        P(("dp", "tensor", "expert"), None, None),
        P(("dp", "tensor", "expert"), None, None),
    )
    return jax.shard_map(shards, mesh=mesh, in_specs=in_specs, out_specs=out_specs, check_vma=False)
```

profile of v0, /device:TPU:1, one launch (start us, length us, event | category | flops | bytes accessed | tf_op | source)
XLA Modules:
  0.0 627.3 jit_solution(496338516431408893)
XLA Ops:
  7.2 0.9 copy.60
  8.5 0.1 copy.62
  8.6 0.2 fusion.22
  8.8 0.1 copy.63
  9.0 1.2 select_reduce_fusion
  10.2 4.3 scatter_custom_fusion
  14.5 0.1 reshape.298
  14.7 0.1 maximum_reduce_fusion
  15.0 16.3 %all_gather.6 = bf16[128,2048]{1,0:T(8,128)(2,1)S(1)} all-gather(bf16[128,512]{1,0:T(8,128)(2,1)S(1)} %copy-done.8), channel_id=1, replica_groups=mesh['dp'=8,'tensor'=8,'expert'=4] {'expert'}, dimensions={1}, use_global_device_ids=true | all-gather | bytes 655360 | tf_op jit(solution)/shard_map/all_gather | solution.py:78
  31.3 4.2 gather_fusion
  35.6 6.1 reshape.310
  41.7 4.5 broadcast_select_fusion
  46.2 15.3 %all-to-all-start = ((bf16[64,12,2048]{2,1,0:T(8,128)(2,1)}), bf16[64,12,2048]{2,1,0:T(8,128)(2,1)}, u32[]{:S(2)}, u32[]{:S(2)}) async-start(bf16[64,12,2048]{2,1,0:T(8,128)(2,1)} %broadcast_select_fusion), calls=%async_computation | async-start | bytes 8388608 | tf_op jit(solution)/shard_map/all_to_all | solution.py:89
  61.5 0.1 copy.77
  61.7 4.3 scatter_custom_fusion.1
  66.0 0.1 reshape.302
  66.2 97.9 %all_gather.7 = bf16[128,2048]{1,0:T(8,128)(2,1)S(1)} all-gather(bf16[128,512]{1,0:T(8,128)(2,1)S(1)} %copy-done.9), channel_id=1, replica_groups=mesh['dp'=8,'tensor'=8,'expert'=4] {'expert'}, dimensions={1}, use_global_device_ids=true | all-gather | bytes 655360 | tf_op jit(solution)/shard_map/all_gather | solution.py:79
  164.1 4.3 gather_fusion.2
  168.4 6.4 %reshape.361 = f32[64,12,2048]{2,1,0:T(8,128)} reshape(bf16[768,2048]{1,0:T(8,128)(2,1)} %gather_fusion.2) | data formatting | bytes 9437184 | tf_op jit(solution)/shard_map/convert_element_type | solution.py:45
  174.8 5.2 select_convert_fusion
  180.1 13.6 %all-to-all-start.2 = ((bf16[64,12,2048]{2,1,0:T(8,128)(2,1)}), bf16[64,12,2048]{2,1,0:T(8,128)(2,1)}, u32[]{:S(2)}, u32[]{:S(2)}) async-start(bf16[64,12,2048]{2,1,0:T(8,128)(2,1)} %select_convert_fusion), calls=%async_computation.3 | async-start | bytes 8388608 | tf_op jit(solution)/shard_map/all_to_all | solution.py:90
  193.7 5.8 fusion.13
  199.6 5.2 fusion.17
  204.8 87.0 %all-to-all-done.2 = bf16[64,12,2048]{2,1,0:T(8,128)(2,1)} async-done(((bf16[64,12,2048]{2,1,0:T(8,128)(2,1)}), bf16[64,12,2048]{2,1,0:T(8,128)(2,1)}, u32[]{:S(2)}, u32[]{:S(2)}) %all-to-all-start.2) | async-done | bytes 3145760 | tf_op jit(solution)/shard_map/all_to_all | solution.py:90
  291.8 6.2 multiply_convert_fusion
  298.0 0.8 copy-done.12
  298.8 3.5 convolution_convert_fusion
  302.4 6.3 %reshape.299 = bf16[64,12,2,1024]{3,2,0,1:T(2,128)(2,1)} reshape(bf16[64,12,2048]{2,0,1:T(8,128)(2,1)} %convolution_convert_fusion) | data formatting | bytes 6291456 | tf_op jit(solution)/shard_map/reshape | solution.py:95
  308.7 1.8 fusion.15
  310.5 3.5 add_convert_fusion
  314.0 6.1 reshape.303
  320.2 27.6 %constant_dynamic-slice_fusion.1 = (bf16[64,12,1,1024]{3,2,0,1:T(2,128)(2,1)}, bf16[64,12,1,1024]{3,2,0,1:T(2,128)(2,1)}, bf16[64,12,1,1024]{3,2,0,1:T(2,128)(2,1)S(1)}, bf16[64,12,1,1024]{3,2,0,1:T(2,128)(2,1)S(1)}) fusion(bf16[64,12,2,1024]{3,2,0,1:T(2,128)(2,1)} %reshape.303, s32[]{:T(128)S(6)} %select_n.147, s32[]{:T(128)S(6)} %select_n.148, ...), kind=kLoop, calls=%fused_computation.96 | loop fusion | bytes 12582920 | tf_op jit(solution)/shard_map/jit(dynamic_index_in_dim)/dynamic_slice | solution.py:98
  347.7 0.6 copy.136
  348.4 33.5 %collective-permute-done = bf16[64,12,1024]{2,0,1:T(8,128)(2,1)S(1)} collective-permute-done((bf16[64,12,1024]{2,0,1:T(8,128)(2,1)S(1)}, bf16[64,12,1024]{2,0,1:T(8,128)(2,1)S(1)}, u32[]{:S(2)}, u32[]{:S(2)}) %collective-permute-start) | collective-permute-done | bytes 1572896 | tf_op jit(solution)/shard_map/ppermute | solution.py:8
  382.0 1.1 fusion.3
  383.1 2.2 copy.71
  385.3 8.7 %all-to-all-start.1 = ((bf16[64,12,1024]{2,1,0:T(8,128)(2,1)}), bf16[64,12,1024]{2,1,0:T(8,128)(2,1)}, u32[]{:S(2)}, u32[]{:S(2)}) async-start(bf16[64,12,1024]{2,1,0:T(8,128)(2,1)} %copy.71), calls=%async_computation.1 | async-start | bytes 4194304 | tf_op jit(solution)/shard_map/all_to_all | solution.py:105
  394.0 2.6 copy.135
  396.8 76.5 %collective-permute-done.1 = bf16[64,12,1024]{2,0,1:T(8,128)(2,1)S(1)} collective-permute-done((bf16[64,12,1024]{2,0,1:T(8,128)(2,1)S(1)}, bf16[64,12,1024]{2,0,1:T(8,128)(2,1)S(1)}, u32[]{:S(2)}, u32[]{:S(2)}) %collective-permute-start.1) | collective-permute-done | bytes 1572896 | tf_op jit(solution)/shard_map/ppermute | solution.py:8
  473.3 1.1 fusion.2
  474.4 2.2 copy.84
  476.6 13.5 %all-to-all-start.3 = ((bf16[64,12,1024]{2,1,0:T(8,128)(2,1)}), bf16[64,12,1024]{2,1,0:T(8,128)(2,1)}, u32[]{:S(2)}, u32[]{:S(2)}) async-start(bf16[64,12,1024]{2,1,0:T(8,128)(2,1)} %copy.84), calls=%async_computation.4 | async-start | bytes 4194304 | tf_op jit(solution)/shard_map/all_to_all | solution.py:106
  490.3 0.1 copy.76
  490.7 2.5 reshape.300
  493.2 5.4 gather_fusion.1
  498.5 2.9 fusion.1
  501.5 0.4 broadcast_in_dim.113
  501.8 0.3 copy.110
  502.2 32.8 %all-to-all-done.3 = bf16[64,12,1024]{2,1,0:T(8,128)(2,1)} async-done(((bf16[64,12,1024]{2,1,0:T(8,128)(2,1)}), bf16[64,12,1024]{2,1,0:T(8,128)(2,1)}, u32[]{:S(2)}, u32[]{:S(2)}) %all-to-all-start.3) | async-done | bytes 1572896 | tf_op jit(solution)/shard_map/all_to_all | solution.py:106
  535.0 2.5 reshape.304
  537.5 5.4 gather_fusion.3
  542.9 2.9 fusion
  545.8 0.4 broadcast_in_dim.119
  546.2 0.3 copy.111
  546.5 1.5 broadcast_select_fusion.1
  548.1 0.3 reduce-scatter.3.cloned.1.call-start
  548.3 0.5 reduce-scatter.3.cloned.1.call-update
  548.9 7.4 %fusion.6 = bf16[1,384,2048]{2,1,0:T(8,128)(2,1)} fusion(bf16[64,12,384]{2,0,1:T(8,128)(2,1)S(1)} %copy-done.13, bf16[64,12,2048]{2,1,0:T(8,128)(2,1)} %all-to-all-done.2), kind=kOutput, calls=%fused_computation.23 | convolution fusion | flops 1208745984 | bytes 5308416 | tf_op jit(solution)/shard_map/smh,smd->hd/dot_general | solution.py:34
  556.3 7.4 %fusion.5 = bf16[1,384,2048]{2,1,0:T(8,128)(2,1)} fusion(bf16[64,12,384]{2,0,1:T(8,128)(2,1)S(1)} %copy-done.7, bf16[64,12,2048]{2,1,0:T(8,128)(2,1)} %all-to-all-done), kind=kOutput, calls=%fused_computation.22 | convolution fusion | flops 1208745984 | bytes 5308416 | tf_op jit(solution)/shard_map/smh,smd->hd/dot_general | solution.py:31
  563.7 7.5 %fusion.4 = bf16[1,384,2048]{2,1,0:T(8,128)(2,1)} fusion(bf16[64,12,384]{2,0,1:T(8,128)(2,1)S(1)} %get-tuple-element.14, bf16[64,12,2048]{2,1,0:T(8,128)(2,1)} %all-to-all-done), kind=kOutput, calls=%fused_computation.21 | convolution fusion | flops 1208745984 | bytes 5308416 | tf_op jit(solution)/shard_map/smh,smd->hd/dot_general | solution.py:28
  571.2 13.1 %reduce-scatter.5.cloned.1.call-done = f32[128,512]{1,0:T(8,128)} async-done(((f32[128,2048]{1,0:T(8,128)}), f32[128,512]{1,0:T(8,128)}) %reduce-scatter.5.cloned.1.call-update) | async-done | bytes 262160 | tf_op jit(solution)/shard_map/reduce_scatter | solution.py:131
  584.4 1.6 convert_element_type.103
  586.0 32.5 %reduce-scatter.3.cloned.1.call-done = f32[128,512]{1,0:T(8,128)} async-done(((f32[128,2048]{1,0:T(8,128)}), f32[128,512]{1,0:T(8,128)}) %reduce-scatter.3.cloned.1.call-update) | async-done | bytes 262160 | tf_op jit(solution)/shard_map/reduce_scatter | solution.py:130
  618.5 1.6 convert_element_type.91
  (57 shorter events, 1.3 us)
Async XLA Ops:
  7.2 284.6 %copy-start = (bf16[1,384,2048]{2,1,0:T(8,128)(2,1)S(1)}, bf16[1,384,2048]{2,1,0:T(8,128)(2,1)}, u32[]{:S(2)}) copy-start(bf16[1,384,2048]{2,1,0:T(8,128)(2,1)} %param.15) | copy-start | bytes 4718596
  7.2 7.8 %copy-start.8 = (bf16[128,512]{1,0:T(8,128)(2,1)S(1)}, bf16[128,512]{1,0:T(8,128)(2,1)}, u32[]{:S(2)}) copy-start(bf16[128,512]{1,0:T(8,128)(2,1)} %param.8) | copy-start | bytes 393220
  46.2 15.3 %copy-start.11 = (f32[128,8]{0,1:T(8,128)S(1)}, f32[128,8]{0,1:T(8,128)}, u32[]{:S(2)}) copy-start(f32[128,8]{0,1:T(8,128)} %param.11) | copy-start | bytes 12292
  46.2 20.0 %copy-start.9 = (bf16[128,512]{1,0:T(8,128)(2,1)S(1)}, bf16[128,512]{1,0:T(8,128)(2,1)}, u32[]{:S(2)}) copy-start(bf16[128,512]{1,0:T(8,128)(2,1)} %param.9) | copy-start | bytes 393220
  46.2 133.9 %all-to-all-start = ((bf16[64,12,2048]{2,1,0:T(8,128)(2,1)}), bf16[64,12,2048]{2,1,0:T(8,128)(2,1)}, u32[]{:S(2)}, u32[]{:S(2)}) async-start(bf16[64,12,2048]{2,1,0:T(8,128)(2,1)} %broadcast_select_fusion), calls=%async_computation | async-start | bytes 8388608 | tf_op jit(solution)/shard_map/all_to_all | solution.py:89
  180.1 111.7 %all-to-all-start.2 = ((bf16[64,12,2048]{2,1,0:T(8,128)(2,1)}), bf16[64,12,2048]{2,1,0:T(8,128)(2,1)}, u32[]{:S(2)}, u32[]{:S(2)}) async-start(bf16[64,12,2048]{2,1,0:T(8,128)(2,1)} %select_convert_fusion), calls=%async_computation.3 | async-start | bytes 8388608 | tf_op jit(solution)/shard_map/all_to_all | solution.py:90
  193.7 5.9 copy-start.3
  298.0 0.8 copy-start.12
  302.4 6.3 %copy-start.4 = (bf16[1,384,2048]{2,1,0:T(8,128)(2,1)S(1)}, bf16[1,384,2048]{2,1,0:T(8,128)(2,1)}, u32[]{:S(2)}) copy-start(bf16[1,384,2048]{2,1,0:T(8,128)(2,1)} %param.13) | copy-start | bytes 4718596
  308.7 1.8 copy-start.5
  308.7 1.8 copy-start.6
  348.3 33.6 %collective-permute-start = (bf16[64,12,1024]{2,0,1:T(8,128)(2,1)S(1)}, bf16[64,12,1024]{2,0,1:T(8,128)(2,1)S(1)}, u32[]{:S(2)}, u32[]{:S(2)}) collective-permute-start(bf16[64,12,1024]{2,0,1:T(8,128)(2,1)S(1)} %bitcast.99), channel_id=1, source_target_pairs={{0,1},{1,0},{2,3},{3,2},{4,5},{5,4},{6,7},{7,6},{8,9},{9,8},{10,11... | collective-permute-start | bytes 4718600 | tf_op jit(solution)/shard_map/ppermute | solution.py:8
  385.3 91.3 %all-to-all-start.1 = ((bf16[64,12,1024]{2,1,0:T(8,128)(2,1)}), bf16[64,12,1024]{2,1,0:T(8,128)(2,1)}, u32[]{:S(2)}, u32[]{:S(2)}) async-start(bf16[64,12,1024]{2,1,0:T(8,128)(2,1)} %copy.71), calls=%async_computation.1 | async-start | bytes 4194304 | tf_op jit(solution)/shard_map/all_to_all | solution.py:105
  394.0 79.3 %copy-start.2 = (bf16[64,12,1,1024]{3,2,0,1:T(2,128)(2,1)S(1)}, bf16[64,12,1,1024]{3,2,0,1:T(2,128)(2,1)}, u32[]{:S(2)}) copy-start(bf16[64,12,1,1024]{3,2,0,1:T(2,128)(2,1)} %get-tuple-element.9) | copy-start | bytes 4718596
  396.7 76.6 %collective-permute-start.1 = (bf16[64,12,1024]{2,0,1:T(8,128)(2,1)S(1)}, bf16[64,12,1024]{2,0,1:T(8,128)(2,1)S(1)}, u32[]{:S(2)}, u32[]{:S(2)}) collective-permute-start(bf16[64,12,1024]{2,0,1:T(8,128)(2,1)S(1)} %bitcast.100), channel_id=1, source_target_pairs={{0,1},{1,0},{2,3},{3,2},{4,5},{5,4},{6,7},{7,6},{8,9},{9,8},{10,11... | collective-permute-start | bytes 4718600 | tf_op jit(solution)/shard_map/ppermute | solution.py:8
  474.4 16.0 %copy-start.10 = (s32[128,8]{0,1:T(8,128)S(1)}, s32[128,8]{0,1:T(8,128)}, u32[]{:S(2)}) copy-start(s32[128,8]{0,1:T(8,128)} %param.10) | copy-start | bytes 12292
  476.6 58.4 %all-to-all-start.3 = ((bf16[64,12,1024]{2,1,0:T(8,128)(2,1)}), bf16[64,12,1024]{2,1,0:T(8,128)(2,1)}, u32[]{:S(2)}, u32[]{:S(2)}) async-start(bf16[64,12,1024]{2,1,0:T(8,128)(2,1)} %copy.84), calls=%async_computation.4 | async-start | bytes 4194304 | tf_op jit(solution)/shard_map/all_to_all | solution.py:106
  490.2 94.2 %reduce-scatter.5.cloned.1.call-start = ((), (), s32[]{:S(2)}) async-start(), calls=%async_computation.7 | async-start | bytes 1310720 | tf_op jit(solution)/shard_map/reduce_scatter | solution.py:131
  546.5 2.3 copy-start.13
  548.1 70.4 %reduce-scatter.3.cloned.1.call-start = ((), (), s32[]{:S(2)}) async-start(), calls=%async_computation.6 | async-start | bytes 1310720 | tf_op jit(solution)/shard_map/reduce_scatter | solution.py:130
  548.9 7.5 %copy-start.7 = (bf16[64,12,384]{2,0,1:T(8,128)(2,1)S(1)}, bf16[64,12,384]{2,0,1:T(8,128)(2,1)}, u32[]{:S(2)}) copy-start(bf16[64,12,384]{2,0,1:T(8,128)(2,1)} %get-tuple-element.13) | copy-start | bytes 1769476
  563.7 56.4 %copy-start.1 = (bf16[1,384,2048]{2,1,0:T(8,128)(2,1)S(1)}, bf16[1,384,2048]{2,1,0:T(8,128)(2,1)}, u32[]{:S(2)}) copy-start(bf16[1,384,2048]{2,1,0:T(8,128)(2,1)} %param.15) | copy-start | bytes 4718596
Sparse Core Ops, SparseCore 0:
  548.2 36.1 reduce-scatter.4
  587.1 31.3 reduce-scatter.2
where the time goes:
time: 635 us; the launch traced here: 627 us
  waiting for transfers between devices  276 us (43%)
  blocking collectives  114 us (18%)
  local copies, waits for them, and re-layouts  97.8 us (15%)
  starting transfers between devices  51.7 us (8%)
  matrix products  48.5 us (8%)
  other arithmetic  24.3 us (4%)
  between operations  14.9 us (2%)
    ppermute x2, waiting for transfers between devices, swapped(): lax.ppermute(x, axis, [(i, i ^ 1 << apart) for i in range(lax.axis_size(a...  110 us
    all_gather x1, blocking collectives, shards(): lax.all_gather(grad_output, 'expert', axis=1, tiled=True)  97.9 us
    all_to_all x1, waiting for transfers between devices, shards(): lax.all_to_all(send_cots, ('dp', 'tensor'), split_axis=0, concat_axis=0,...  87 us
    all_to_all x1, waiting for transfers between devices, shards(): lax.all_to_all(input_slot, ('dp', 'tensor'), split_axis=0, concat_axis=0,...  32.8 us
    reduce_scatter x1, waiting for transfers between devices, shards(): lax.psum_scatter(placed_out, 'expert', scatter_dimension=1, tiled=True)  32.5 us
    dynamic_slice x1, local copies, waits for them, and re-layouts, shards(): mine_in = lax.dynamic_index_in_dim(in_split, half_index, 2, keepdims=False)  27.6 us
    all_gather x1, blocking collectives, shards(): lax.all_gather(moe_input, 'expert', axis=1, tiled=True)  16.3 us
    all_to_all x1, starting transfers between devices, shards(): lax.all_to_all(send_rows, ('dp', 'tensor'), split_axis=0, concat_axis=0,...  15.3 us
  transfers between devices with their start and end apart: 8, of which 6 were waited for; matrix products, arithmetic and copies ran while one was open for 12% of the time, Pallas kernels for 0%

commit v1 on v0

--- a/solution.py
+++ b/solution.py
@@ -76,7 +76,12 @@
     slot_weight = jnp.zeros((slot_count,), jnp.float32).at[pair_place].set(flat_weight, mode="drop")
     whole_input, whole_cot = (
         lax.all_gather(moe_input, "expert", axis=1, tiled=True),
-        lax.all_gather(grad_output, "expert", axis=1, tiled=True),
+        jnp.concatenate(
+            lax.all_to_all(
+                jnp.stack([grad_output] * lax.axis_size("expert"), axis=0), "expert", 0, 0
+            ),
+            1,
+        ),
     )
     owners = lax.dynamic_index_in_dim(
         slot_owner.reshape(groups, 2, slot_depth), parity, 1, keepdims=False

time: 635 us -> 610 us (0.961)
  blocking collectives: 114 us -> 15.3 us
  starting transfers between devices: 51.7 us -> 95.8 us
  waiting for transfers between devices: 276 us -> 305 us
    all_gather x1 -> x0, blocking collectives: 97.9 us -> none  [shards(): lax.all_gather(grad_output, 'expert', axis=1, tiled=True)]
    all_to_all x1, waiting for transfers between devices: 0.01 us -> 74.5 us  [shards(): lax.all_to_all(send_rows, ('dp', 'tensor'), split_axis=0, concat_axis=0,...]
    all_to_all x1, waiting for transfers between devices: 87 us -> 43.9 us  [shards(): lax.all_to_all(send_cots, ('dp', 'tensor'), split_axis=0, concat_axis=0,...]
    ppermute x2, starting transfers between devices: 0.19 us -> 38.6 us  [swapped(): lax.ppermute(x, axis, [(i, i ^ 1 << apart) for i in range(lax.axis_size(a...]
    all_to_all x0 -> x1, starting transfers between devices: none -> 6.44 us  [shards(): lax.all_to_all(jnp.stack([grad_output] * lax.axis_size('expert'), axis=0)...]
  transfers between devices with their start and end apart: 8 -> 9, of which waited for: 6 -> 7; matrix products, arithmetic and copies ran while one was open for 12% -> 16% of each run, Pallas kernels for 0% -> 0%
where the time goes in v1:
time: 610 us; the launch traced here: 602 us
  waiting for transfers between devices  305 us (50%)
  local copies, waits for them, and re-layouts  99.5 us (16%)
  starting transfers between devices  95.8 us (16%)
  matrix products  47.7 us (8%)
  other arithmetic  23.6 us (4%)
  blocking collectives  15.3 us (3%)
  between operations  14.9 us (2%)
    ppermute x2, waiting for transfers between devices, swapped(): lax.ppermute(x, axis, [(i, i ^ 1 << apart) for i in range(lax.axis_size(a...  108 us
    all_to_all x1, waiting for transfers between devices, shards(): lax.all_to_all(send_rows, ('dp', 'tensor'), split_axis=0, concat_axis=0,...  74.5 us
    all_to_all x1, waiting for transfers between devices, shards(): lax.all_to_all(send_cots, ('dp', 'tensor'), split_axis=0, concat_axis=0,...  43.9 us
    ppermute x2, starting transfers between devices, swapped(): lax.ppermute(x, axis, [(i, i ^ 1 << apart) for i in range(lax.axis_size(a...  38.6 us
    all_to_all x1, waiting for transfers between devices, shards(): lax.all_to_all(input_slot, ('dp', 'tensor'), split_axis=0, concat_axis=0,...  37.6 us
    reduce_scatter x1, waiting for transfers between devices, shards(): lax.psum_scatter(placed_out, 'expert', scatter_dimension=1, tiled=True)  32.5 us
    dynamic_slice x1, local copies, waits for them, and re-layouts, shards(): mine_in = lax.dynamic_index_in_dim(in_split, half_index, 2, keepdims=False)  27.5 us
    all_to_all x1, starting transfers between devices, shards(): lax.all_to_all(send_rows, ('dp', 'tensor'), split_axis=0, concat_axis=0,...  15.4 us
  transfers between devices with their start and end apart: 9, of which 7 were waited for; matrix products, arithmetic and copies ran while one was open for 16% of the time, Pallas kernels for 0%

profile of v1, /device:TPU:1, one launch (start us, length us, event | category | flops | bytes accessed | tf_op | source)
XLA Modules:
  0.0 601.5 jit_solution(16592551732129783403)
XLA Ops:
  7.2 1.9 stack.2
  9.1 6.4 %all-to-all-start.2 = ((bf16[4,128,512]{2,1,0:T(8,128)(2,1)}), bf16[4,128,512]{2,1,0:T(8,128)(2,1)S(1)}, u32[]{:S(2)}, u32[]{:S(2)}) async-start(bf16[4,128,512]{2,1,0:T(8,128)(2,1)} %stack.2), calls=%async_computation.3 | async-start | bytes 1048576 | tf_op jit(solution)/shard_map/all_to_all | solution.py:80
  15.5 0.8 copy.60
  16.7 0.2 fusion.22
  17.1 0.5 select_reduce_fusion
  17.7 4.3 scatter_custom_fusion
  22.0 0.1 reshape.306
  22.2 15.3 %all_gather.3 = bf16[128,2048]{1,0:T(8,128)(2,1)S(1)} all-gather(bf16[128,512]{1,0:T(8,128)(2,1)S(1)} %copy-done.8), channel_id=1, replica_groups=mesh['dp'=8,'tensor'=8,'expert'=4] {'expert'}, dimensions={1}, use_global_device_ids=true | all-gather | bytes 655360 | tf_op jit(solution)/shard_map/all_gather | solution.py:78
  37.8 4.2 gather_fusion
  42.1 6.1 %reshape.320 = bf16[64,12,2048]{2,1,0:T(8,128)(2,1)} reshape(bf16[768,2048]{1,0:T(8,128)(2,1)} %gather_fusion) | data formatting | bytes 6291456 | tf_op jit(solution)/shard_map/gather | solution.py:43
  48.2 4.5 broadcast_select_fusion
  52.7 15.4 %all-to-all-start = ((bf16[64,12,2048]{2,1,0:T(8,128)(2,1)}), bf16[64,12,2048]{2,1,0:T(8,128)(2,1)}, u32[]{:S(2)}, u32[]{:S(2)}) async-start(bf16[64,12,2048]{2,1,0:T(8,128)(2,1)} %broadcast_select_fusion), calls=%async_computation | async-start | bytes 8388608 | tf_op jit(solution)/shard_map/all_to_all | solution.py:94
  68.4 4.3 scatter_custom_fusion.1
  72.7 0.1 reshape.310
  72.9 4.3 gather_fusion.2
  77.3 6.4 %reshape.371 = f32[64,12,2048]{2,1,0:T(8,128)} reshape(bf16[768,2048]{1,0:T(8,128)(2,1)} %gather_fusion.2) | data formatting | bytes 9437184 | tf_op jit(solution)/shard_map/convert_element_type | solution.py:45
  83.7 5.2 select_convert_fusion
  88.9 74.5 %all-to-all-done = bf16[64,12,2048]{2,1,0:T(8,128)(2,1)} async-done(((bf16[64,12,2048]{2,1,0:T(8,128)(2,1)}), bf16[64,12,2048]{2,1,0:T(8,128)(2,1)}, u32[]{:S(2)}, u32[]{:S(2)}) %all-to-all-start) | async-done | bytes 3145760 | tf_op jit(solution)/shard_map/all_to_all | solution.py:94
  163.4 8.2 %all-to-all-start.3 = ((bf16[64,12,2048]{2,1,0:T(8,128)(2,1)}), bf16[64,12,2048]{2,1,0:T(8,128)(2,1)}, u32[]{:S(2)}, u32[]{:S(2)}) async-start(bf16[64,12,2048]{2,1,0:T(8,128)(2,1)} %select_convert_fusion), calls=%async_computation.4 | async-start | bytes 8388608 | tf_op jit(solution)/shard_map/all_to_all | solution.py:95
  171.6 5.8 fusion.13
  177.5 5.2 fusion.17
  182.7 43.9 %all-to-all-done.3 = bf16[64,12,2048]{2,1,0:T(8,128)(2,1)} async-done(((bf16[64,12,2048]{2,1,0:T(8,128)(2,1)}), bf16[64,12,2048]{2,1,0:T(8,128)(2,1)}, u32[]{:S(2)}, u32[]{:S(2)}) %all-to-all-start.3) | async-done | bytes 3145760 | tf_op jit(solution)/shard_map/all_to_all | solution.py:95
  226.6 5.4 multiply_convert_fusion
  232.0 0.8 copy-done.12
  232.8 3.5 convolution_convert_fusion
  236.3 6.3 %reshape.307 = bf16[64,12,2,1024]{3,2,0,1:T(2,128)(2,1)} reshape(bf16[64,12,2048]{2,0,1:T(8,128)(2,1)} %convolution_convert_fusion) | data formatting | bytes 6291456 | tf_op jit(solution)/shard_map/reshape | solution.py:100
  242.6 1.8 fusion.15
  244.5 3.5 add_convert_fusion
  248.0 6.1 %reshape.313 = bf16[64,12,2,1024]{3,2,0,1:T(2,128)(2,1)} reshape(bf16[64,12,2048]{2,0,1:T(8,128)(2,1)} %add_convert_fusion) | data formatting | bytes 6291456 | tf_op jit(solution)/shard_map/reshape | solution.py:101
  254.1 27.5 %constant_dynamic-slice_fusion.1 = (bf16[64,12,1,1024]{3,2,0,1:T(2,128)(2,1)}, bf16[64,12,1,1024]{3,2,0,1:T(2,128)(2,1)}, bf16[64,12,1,1024]{3,2,0,1:T(2,128)(2,1)S(1)}, bf16[64,12,1,1024]{3,2,0,1:T(2,128)(2,1)S(1)}) fusion(bf16[64,12,2,1024]{3,2,0,1:T(2,128)(2,1)} %reshape.313, s32[]{:T(128)S(6)} %select_n.147, s32[]{:T(128)S(6)} %select_n.148, ...), kind=kLoop, calls=%fused_computation.96 | loop fusion | bytes 12582920 | tf_op jit(solution)/shard_map/jit(dynamic_index_in_dim)/dynamic_slice | solution.py:103
  281.6 0.6 copy.138
  282.2 37.1 %collective-permute-start = (bf16[64,12,1024]{2,0,1:T(8,128)(2,1)S(1)}, bf16[64,12,1024]{2,0,1:T(8,128)(2,1)S(1)}, u32[]{:S(2)}, u32[]{:S(2)}) collective-permute-start(bf16[64,12,1024]{2,0,1:T(8,128)(2,1)S(1)} %bitcast.104), channel_id=1, source_target_pairs={{0,1},{1,0},{2,3},{3,2},{4,5},{5,4},{6,7},{7,6},{8,9},{9,8},{10,11... | collective-permute-start | bytes 4718600 | tf_op jit(solution)/shard_map/ppermute | solution.py:8
  319.3 31.5 %collective-permute-done = bf16[64,12,1024]{2,0,1:T(8,128)(2,1)S(1)} collective-permute-done((bf16[64,12,1024]{2,0,1:T(8,128)(2,1)S(1)}, bf16[64,12,1024]{2,0,1:T(8,128)(2,1)S(1)}, u32[]{:S(2)}, u32[]{:S(2)}) %collective-permute-start) | collective-permute-done | bytes 1572896 | tf_op jit(solution)/shard_map/ppermute | solution.py:8
  350.8 1.1 fusion.3
  351.9 2.2 copy.71
  354.1 13.4 %all-to-all-start.1 = ((bf16[64,12,1024]{2,1,0:T(8,128)(2,1)}), bf16[64,12,1024]{2,1,0:T(8,128)(2,1)}, u32[]{:S(2)}, u32[]{:S(2)}) async-start(bf16[64,12,1024]{2,1,0:T(8,128)(2,1)} %copy.71), calls=%async_computation.1 | async-start | bytes 4194304 | tf_op jit(solution)/shard_map/all_to_all | solution.py:110
  367.5 2.6 copy.137
  370.1 1.5 collective-permute-start.1
  371.7 76.4 %collective-permute-done.1 = bf16[64,12,1024]{2,0,1:T(8,128)(2,1)S(1)} collective-permute-done((bf16[64,12,1024]{2,0,1:T(8,128)(2,1)S(1)}, bf16[64,12,1024]{2,0,1:T(8,128)(2,1)S(1)}, u32[]{:S(2)}, u32[]{:S(2)}) %collective-permute-start.1) | collective-permute-done | bytes 1572896 | tf_op jit(solution)/shard_map/ppermute | solution.py:8
  448.0 1.1 fusion.2
  449.1 2.2 copy.85
  451.3 13.4 %all-to-all-start.4 = ((bf16[64,12,1024]{2,1,0:T(8,128)(2,1)}), bf16[64,12,1024]{2,1,0:T(8,128)(2,1)}, u32[]{:S(2)}, u32[]{:S(2)}) async-start(bf16[64,12,1024]{2,1,0:T(8,128)(2,1)} %copy.85), calls=%async_computation.5 | async-start | bytes 4194304 | tf_op jit(solution)/shard_map/all_to_all | solution.py:111
  465.0 0.1 copy.76
  465.3 2.5 reshape.308
  467.8 5.4 gather_fusion.1
  473.2 2.9 fusion.1
  476.1 0.4 broadcast_in_dim.113
  476.5 0.3 copy.112
  476.8 37.6 %all-to-all-done.4 = bf16[64,12,1024]{2,1,0:T(8,128)(2,1)} async-done(((bf16[64,12,1024]{2,1,0:T(8,128)(2,1)}), bf16[64,12,1024]{2,1,0:T(8,128)(2,1)}, u32[]{:S(2)}, u32[]{:S(2)}) %all-to-all-start.4) | async-done | bytes 1572896 | tf_op jit(solution)/shard_map/all_to_all | solution.py:111
  514.4 2.5 reshape.314
  516.9 5.4 gather_fusion.3
  522.3 2.9 fusion
  525.2 0.4 broadcast_in_dim.119
  525.6 0.3 copy.113
  526.0 1.5 broadcast_select_fusion.1
  527.5 0.3 reduce-scatter.3.cloned.1.call-start
  527.8 0.5 reduce-scatter.3.cloned.1.call-update
  528.3 7.5 %fusion.6 = bf16[1,384,2048]{2,1,0:T(8,128)(2,1)} fusion(bf16[64,12,384]{2,0,1:T(8,128)(2,1)S(1)} %copy-done.13, bf16[64,12,2048]{2,1,0:T(8,128)(2,1)} %all-to-all-done.3), kind=kOutput, calls=%fused_computation.23 | convolution fusion | flops 1208745984 | bytes 5308416 | tf_op jit(solution)/shard_map/smh,smd->hd/dot_general | solution.py:34
  535.8 7.4 %fusion.5 = bf16[1,384,2048]{2,1,0:T(8,128)(2,1)} fusion(bf16[64,12,384]{2,0,1:T(8,128)(2,1)S(1)} %copy-done.7, bf16[64,12,2048]{2,1,0:T(8,128)(2,1)} %all-to-all-done), kind=kOutput, calls=%fused_computation.22 | convolution fusion | flops 1208745984 | bytes 5308416 | tf_op jit(solution)/shard_map/smh,smd->hd/dot_general | solution.py:31
  543.2 7.5 %fusion.4 = bf16[1,384,2048]{2,1,0:T(8,128)(2,1)} fusion(bf16[64,12,384]{2,0,1:T(8,128)(2,1)S(1)} %get-tuple-element.14, bf16[64,12,2048]{2,1,0:T(8,128)(2,1)} %all-to-all-done), kind=kOutput, calls=%fused_computation.21 | convolution fusion | flops 1208745984 | bytes 5308416 | tf_op jit(solution)/shard_map/smh,smd->hd/dot_general | solution.py:28
  550.7 7.9 %reduce-scatter.5.cloned.1.call-done = f32[128,512]{1,0:T(8,128)} async-done(((f32[128,2048]{1,0:T(8,128)}), f32[128,512]{1,0:T(8,128)}) %reduce-scatter.5.cloned.1.call-update) | async-done | bytes 262160 | tf_op jit(solution)/shard_map/reduce_scatter | solution.py:136
  558.6 1.6 convert_element_type.103
  560.2 32.5 %reduce-scatter.3.cloned.1.call-done = f32[128,512]{1,0:T(8,128)} async-done(((f32[128,2048]{1,0:T(8,128)}), f32[128,512]{1,0:T(8,128)}) %reduce-scatter.3.cloned.1.call-update) | async-done | bytes 262160 | tf_op jit(solution)/shard_map/reduce_scatter | solution.py:135
  592.7 1.6 convert_element_type.91
  (60 shorter events, 1.6 us)
Async XLA Ops:
  7.2 219.4 %copy-start = (bf16[1,384,2048]{2,1,0:T(8,128)(2,1)S(1)}, bf16[1,384,2048]{2,1,0:T(8,128)(2,1)}, u32[]{:S(2)}) copy-start(bf16[1,384,2048]{2,1,0:T(8,128)(2,1)} %param.15) | copy-start | bytes 4718596
  7.2 9.9 %copy-start.11 = (s32[128]{0:T(128)S(1)}, s32[128]{0:T(128)}, u32[]{:S(2)}) copy-start(s32[128]{0:T(128)} %param.12) | copy-start | bytes 1540
  7.2 15.0 %copy-start.8 = (bf16[128,512]{1,0:T(8,128)(2,1)S(1)}, bf16[128,512]{1,0:T(8,128)(2,1)}, u32[]{:S(2)}) copy-start(bf16[128,512]{1,0:T(8,128)(2,1)} %param.8) | copy-start | bytes 393220
  9.1 43.7 %all-to-all-start.2 = ((bf16[4,128,512]{2,1,0:T(8,128)(2,1)}), bf16[4,128,512]{2,1,0:T(8,128)(2,1)S(1)}, u32[]{:S(2)}, u32[]{:S(2)}) async-start(bf16[4,128,512]{2,1,0:T(8,128)(2,1)} %stack.2), calls=%async_computation.3 | async-start | bytes 1048576 | tf_op jit(solution)/shard_map/all_to_all | solution.py:80
  52.7 15.4 %copy-start.10 = (f32[128,8]{0,1:T(8,128)S(1)}, f32[128,8]{0,1:T(8,128)}, u32[]{:S(2)}) copy-start(f32[128,8]{0,1:T(8,128)} %param.11) | copy-start | bytes 12292
  52.7 110.6 %all-to-all-start = ((bf16[64,12,2048]{2,1,0:T(8,128)(2,1)}), bf16[64,12,2048]{2,1,0:T(8,128)(2,1)}, u32[]{:S(2)}, u32[]{:S(2)}) async-start(bf16[64,12,2048]{2,1,0:T(8,128)(2,1)} %broadcast_select_fusion), calls=%async_computation | async-start | bytes 8388608 | tf_op jit(solution)/shard_map/all_to_all | solution.py:94
  163.4 63.2 %all-to-all-start.3 = ((bf16[64,12,2048]{2,1,0:T(8,128)(2,1)}), bf16[64,12,2048]{2,1,0:T(8,128)(2,1)}, u32[]{:S(2)}, u32[]{:S(2)}) async-start(bf16[64,12,2048]{2,1,0:T(8,128)(2,1)} %select_convert_fusion), calls=%async_computation.4 | async-start | bytes 8388608 | tf_op jit(solution)/shard_map/all_to_all | solution.py:95
  171.6 5.9 copy-start.3
  232.0 0.8 copy-start.12
  232.0 12.4 %copy-start.6 = (bf16[64,12,384]{2,0,1:T(8,128)(2,1)}, bf16[64,12,384]{2,0,1:T(8,128)(2,1)S(1)}, u32[]{:S(2)}) copy-start(bf16[64,12,384]{2,0,1:T(8,128)(2,1)S(1)} %get-tuple-element.13) | copy-start | bytes 1769476
  236.3 6.3 %copy-start.4 = (bf16[1,384,2048]{2,1,0:T(8,128)(2,1)S(1)}, bf16[1,384,2048]{2,1,0:T(8,128)(2,1)}, u32[]{:S(2)}) copy-start(bf16[1,384,2048]{2,1,0:T(8,128)(2,1)} %param.13) | copy-start | bytes 4718596
  242.6 1.8 copy-start.5
  282.2 68.5 %collective-permute-start = (bf16[64,12,1024]{2,0,1:T(8,128)(2,1)S(1)}, bf16[64,12,1024]{2,0,1:T(8,128)(2,1)S(1)}, u32[]{:S(2)}, u32[]{:S(2)}) collective-permute-start(bf16[64,12,1024]{2,0,1:T(8,128)(2,1)S(1)} %bitcast.104), channel_id=1, source_target_pairs={{0,1},{1,0},{2,3},{3,2},{4,5},{5,4},{6,7},{7,6},{8,9},{9,8},{10,11... | collective-permute-start | bytes 4718600 | tf_op jit(solution)/shard_map/ppermute | solution.py:8
  354.1 97.3 %all-to-all-start.1 = ((bf16[64,12,1024]{2,1,0:T(8,128)(2,1)}), bf16[64,12,1024]{2,1,0:T(8,128)(2,1)}, u32[]{:S(2)}, u32[]{:S(2)}) async-start(bf16[64,12,1024]{2,1,0:T(8,128)(2,1)} %copy.71), calls=%async_computation.1 | async-start | bytes 4194304 | tf_op jit(solution)/shard_map/all_to_all | solution.py:110
  367.5 80.6 %copy-start.2 = (bf16[64,12,1,1024]{3,2,0,1:T(2,128)(2,1)S(1)}, bf16[64,12,1,1024]{3,2,0,1:T(2,128)(2,1)}, u32[]{:S(2)}) copy-start(bf16[64,12,1,1024]{3,2,0,1:T(2,128)(2,1)} %get-tuple-element.9) | copy-start | bytes 4718596
  370.1 77.9 %collective-permute-start.1 = (bf16[64,12,1024]{2,0,1:T(8,128)(2,1)S(1)}, bf16[64,12,1024]{2,0,1:T(8,128)(2,1)S(1)}, u32[]{:S(2)}, u32[]{:S(2)}) collective-permute-start(bf16[64,12,1024]{2,0,1:T(8,128)(2,1)S(1)} %bitcast.105), channel_id=1, source_target_pairs={{0,1},{1,0},{2,3},{3,2},{4,5},{5,4},{6,7},{7,6},{8,9},{9,8},{10,11... | collective-permute-start | bytes 4718600 | tf_op jit(solution)/shard_map/ppermute | solution.py:8
  449.1 15.8 %copy-start.9 = (s32[128,8]{0,1:T(8,128)S(1)}, s32[128,8]{0,1:T(8,128)}, u32[]{:S(2)}) copy-start(s32[128,8]{0,1:T(8,128)} %param.10) | copy-start | bytes 12292
  451.3 63.1 %all-to-all-start.4 = ((bf16[64,12,1024]{2,1,0:T(8,128)(2,1)}), bf16[64,12,1024]{2,1,0:T(8,128)(2,1)}, u32[]{:S(2)}, u32[]{:S(2)}) async-start(bf16[64,12,1024]{2,1,0:T(8,128)(2,1)} %copy.85), calls=%async_computation.5 | async-start | bytes 4194304 | tf_op jit(solution)/shard_map/all_to_all | solution.py:111
  464.8 93.8 %reduce-scatter.5.cloned.1.call-start = ((), (), s32[]{:S(2)}) async-start(), calls=%async_computation.8 | async-start | bytes 1310720 | tf_op jit(solution)/shard_map/reduce_scatter | solution.py:136
  525.9 2.3 copy-start.13
  527.5 65.2 %reduce-scatter.3.cloned.1.call-start = ((), (), s32[]{:S(2)}) async-start(), calls=%async_computation.7 | async-start | bytes 1310720 | tf_op jit(solution)/shard_map/reduce_scatter | solution.py:135
  528.3 7.5 %copy-start.7 = (bf16[64,12,384]{2,0,1:T(8,128)(2,1)S(1)}, bf16[64,12,384]{2,0,1:T(8,128)(2,1)}, u32[]{:S(2)}) copy-start(bf16[64,12,384]{2,0,1:T(8,128)(2,1)} %copy-done.6) | copy-start | bytes 1769476
  543.2 51.1 %copy-start.1 = (bf16[1,384,2048]{2,1,0:T(8,128)(2,1)S(1)}, bf16[1,384,2048]{2,1,0:T(8,128)(2,1)}, u32[]{:S(2)}) copy-start(bf16[1,384,2048]{2,1,0:T(8,128)(2,1)} %param.15) | copy-start | bytes 4718596
Sparse Core Ops, SparseCore 0:
  527.6 30.9 reduce-scatter.4
  561.3 31.3 reduce-scatter.2
